TPU v7x, 32 devices: a whole 2x2x4 slice. The times are simulated.
32 devices in a mesh: row: 8 (over z, x), col: 4 (over y, core).
Axes of the slice: x: 2, y: 2, z: 4, core: 2. Of those that a mesh axis runs over, the one named last changes fastest.
Arguments:
- coeffs: float32 [4096, 4096], P('row', 'col'), may hold values from -6 to 6
- ham_alpha: float32 [4096, 4096], P('row'), may hold values from -1.5 to 7.5, as said below
- ham_beta: float32 [4096, 4096], P('col'), may hold values from -1.5 to 7.5, as said below
Outputs:
- sigma_vec: float32 [4096, 4096], P('row', 'col')
Inputs may be any that keep to these rules, and one draw needn't show every extreme that they name: `ham_alpha`: symmetric. `ham_beta`: symmetric.
All inputs are finite; a program needn't handle non-finite values.
Results may differ from a plain program's by a relative error of at most 0.00005.
Values sent between devices are 32-bit elements; how exact they have to be, the bound alone decides.
A program may use at most 128 MiB of HBM per device.

v0:
```python
import jax
import jax.numpy as jnp
from jax import lax
from jax.sharding import PartitionSpec as P

HIGHEST = lax.Precision.HIGHEST


def local(coeffs, ham_alpha, ham_beta):
    ham_cols = ham_alpha
    alpha_part = jnp.dot(
        ham_cols,
        lax.all_gather(coeffs, "row", axis=0, tiled=True),
        precision=HIGHEST,
        preferred_element_type=jnp.float32,
    )
    ham_cols = ham_beta
    flipped = lax.psum_scatter(
        lax.dot_general(
            ham_cols,
            coeffs,
            (((0,), (1,)), ((), ())),
            precision=HIGHEST,
            preferred_element_type=jnp.float32,
        ),
        "col",
        scatter_dimension=0,
        tiled=True,
    )
    beta_part = flipped.T
    return alpha_part + beta_part


def solution(mesh):
    in_specs = (P("row", "col"), P("row", None), P("col", None))
    out_specs = P("row", "col")
    return jax.shard_map(local, mesh=mesh, in_specs=in_specs, out_specs=out_specs, check_vma=False)
```

profile of v0, /device:TPU:0, one launch (start us, length us, event | category | flops | bytes accessed | tf_op | source)
XLA Modules:
  0.0 311.4 jit_solution(360071280778495948)
XLA Ops:
  7.4 0.0 reduce-scatter.2.cloned.1.call-start
  7.4 31.3 %fusion = f32[4096,512]{0,1:T(8,128)} fusion(f32[1024,4096]{1,0:T(8,128)} %param.5, f32[512,1024]{1,0:T(8,128)} %param.3), kind=kOutput, calls=%fused_computation.1 | convolution fusion | flops 25769803776 | bytes 27262976 | tf_op jit(solution)/shard_map/dot_general | solution.py:19
  38.7 0.0 reduce-scatter.2.cloned.1.call-update
  38.7 0.2 all-gather.2.cloned.1.call-start
  39.0 0.3 all-gather.2.cloned.1.call-update
  39.3 73.5 %reduce-scatter.2.cloned.1.call-done = f32[1024,512]{0,1:T(8,128)} async-done(((f32[4096,512]{0,1:T(8,128)}), f32[1024,512]{0,1:T(8,128)}) %reduce-scatter.2.cloned.1.call-update) | async-done | bytes 2097168 | tf_op jit(solution)/shard_map/reduce_scatter | solution.py:18
  112.8 158.3 %all-gather.2.cloned.1.call-done = f32[4096,1024]{1,0:T(8,128)} async-done(((f32[512,1024]{1,0:T(8,128)}), f32[4096,1024]{1,0:T(8,128)}) %all-gather.2.cloned.1.call-update) | async-done | bytes 16777232 | tf_op jit(solution)/shard_map/all_gather | solution.py:13
  271.2 32.7 %bitcast_add_fusion = f32[512,1024]{1,0:T(8,128)} fusion(f32[1024,512]{0,1:T(8,128)} %reduce-scatter.2.cloned.1.call-done, f32[512,4096]{1,0:T(8,128)} %param.4, f32[4096,1024]{1,0:T(8,128)} %all-gather.2.cloned.1.call-done), kind=kOutput, calls=%fused_computation | convolution fusion | flops 25770328064 | bytes 29360128 | tf_op jit(solution)/shard_map/dot_general | solution.py:11
Async XLA Ops:
  7.4 105.5 %reduce-scatter.2.cloned.1.call-start = ((), (), s32[]{:S(2)}) async-start(), calls=%async_computation.2 | async-start | bytes 10485760 | tf_op jit(solution)/shard_map/reduce_scatter | solution.py:18
  38.7 232.5 %all-gather.2.cloned.1.call-start = ((), (), s32[]{:S(2)}) async-start(), calls=%async_computation.1 | async-start | bytes 18874368 | tf_op jit(solution)/shard_map/all_gather | solution.py:13
Sparse Core Ops, SparseCore 0:
  38.8 73.9 reduce-scatter.1
Sparse Core Ops, SparseCore 1:
  41.3 229.8 all-gather.1
where the time goes:
time: 312 us; the launch traced here: 311 us
  waiting for transfers between devices  232 us (74%)
  matrix products  64.1 us (21%)
  between operations  14.8 us (5%)
    all_gather x1, waiting for transfers between devices, local(): lax.all_gather(coeffs, 'row', axis=0, tiled=True)  158 us
    reduce_scatter x1, waiting for transfers between devices, local(): lax.psum_scatter(lax.dot_general(ham_cols, coeffs, (((0,), (1,)), ((), ()...  73.5 us
    dot_general x1, matrix products, local(): jnp.dot(ham_cols, lax.all_gather(coeffs, 'row', axis=0, tiled=True), prec...  32.7 us
    dot_general x1, matrix products, local(): lax.dot_general(ham_cols, coeffs, (((0,), (1,)), ((), ())), precision=HIG...  31.3 us
  transfers between devices with their start and end apart: 2, of which 2 were waited for; matrix products, arithmetic and copies ran while one was open for 0% of the time, Pallas kernels for 0%

commit v1 on v0

--- a/solution.py
+++ b/solution.py
@@ -2,17 +2,35 @@
 import jax.numpy as jnp
 from jax import lax
 from jax.sharding import PartitionSpec as P
+from jax.lax import axis_index, axis_size, ppermute
 
 HIGHEST = lax.Precision.HIGHEST
+
+
+def _place_kinds(m):
+    arr_now = axis_size("row")
+    far_arr = axis_index("row")
+    small, arr_out, z = (arr_now, far_arr, m.shape[0])
+    local_next = lax.dynamic_update_slice_in_dim(
+        jnp.zeros(tuple((at * small if jj == 0 else at for jj, at in enumerate(m.shape))), m.dtype),
+        m,
+        arr_out * z,
+        axis=0,
+    )
+    ix = 1
+    while ix < small:
+        m = ppermute(m, "row", tuple(((jj, (jj + 1) % small) for jj in range(small))))
+        local_next = lax.dynamic_update_slice_in_dim(
+            local_next, m, (arr_out - ix) % small * z, axis=0
+        )
+        ix = ix + 1
+    return local_next
 
 
 def local(coeffs, ham_alpha, ham_beta):
     ham_cols = ham_alpha
     alpha_part = jnp.dot(
-        ham_cols,
-        lax.all_gather(coeffs, "row", axis=0, tiled=True),
-        precision=HIGHEST,
-        preferred_element_type=jnp.float32,
+        ham_cols, _place_kinds(coeffs), precision=HIGHEST, preferred_element_type=jnp.float32
     )
     ham_cols = ham_beta
     flipped = lax.psum_scatter(

time: 312 us -> 475 us (1.52)
  waiting for transfers between devices: 232 us -> 312 us
  matrix products: 64.1 us -> 114 us
  local copies, waits for them, and re-layouts: 0 us -> 32.6 us
    ppermute x0 -> x7, waiting for transfers between devices: none -> 312 us  [_place_kinds(): ppermute(m, 'row', tuple(((jj, (jj + 1) % small) for jj in range(small))))]
    all_gather x1 -> x0, waiting for transfers between devices: 158 us -> none  [local(): lax.all_gather(coeffs, 'row', axis=0, tiled=True)]
    reduce_scatter x1, waiting for transfers between devices: 73.5 us -> 0.01 us  [local(): lax.psum_scatter(lax.dot_general(ham_cols, coeffs, (((0,), (1,)), ((), ()...]
    dot_general x1, matrix products: 31.3 us -> 57.6 us  [local(): lax.dot_general(ham_cols, coeffs, (((0,), (1,)), ((), ())), precision=HIG...]
    dot_general x1, matrix products: 32.7 us -> 56.3 us  [local(): jnp.dot(ham_cols, _place_kinds(coeffs), precision=HIGHEST, preferred_elem...]
    dynamic_update_slice x0 -> x8, local copies, waits for them, and re-layouts: none -> 15.3 us  [the longest x7 13.8 us: _place_kinds(): lax.dynamic_update_slice_in_dim(local_next, m, (arr_out - ix) % small * z...]
    broadcast_in_dim x0 -> x1, local copies, waits for them, and re-layouts: none -> 8.74 us  [_place_kinds(): jnp.zeros(tuple((at * small if jj == 0 else at for jj, at in enumerate(m....]
    unnamed x0 -> x22, local copies, waits for them, and re-layouts: none -> 6.67 us
  transfers between devices with their start and end apart: 2 -> 8, of which waited for: 2 -> 7; matrix products, arithmetic and copies ran while one was open for 0% -> 5% of each run, Pallas kernels for 0% -> 0%
where the time goes in v1:
time: 475 us
  waiting for transfers between devices  312 us (66%)
  matrix products  114 us (24%)
  local copies, waits for them, and re-layouts  32.6 us (7%)
  between operations  13.4 us (3%)
    ppermute x7, waiting for transfers between devices, _place_kinds(): ppermute(m, 'row', tuple(((jj, (jj + 1) % small) for jj in range(small))))  312 us
    dot_general x1, matrix products, local(): lax.dot_general(ham_cols, coeffs, (((0,), (1,)), ((), ())), precision=HIG...  57.6 us
    dot_general x1, matrix products, local(): jnp.dot(ham_cols, _place_kinds(coeffs), precision=HIGHEST, preferred_elem...  56.3 us
    dynamic_update_slice x7, local copies, waits for them, and re-layouts, _place_kinds(): lax.dynamic_update_slice_in_dim(local_next, m, (arr_out - ix) % small * z...  13.8 us
  transfers between devices with their start and end apart: 8, of which 7 were waited for; matrix products, arithmetic and copies ran while one was open for 5% of the time, Pallas kernels for 0%

profile of v1, /device:TPU:0, one launch (start us, length us, event | category | flops | bytes accessed | tf_op | source)
XLA Modules:
  0.0 475.2 jit_solution(5197545258428441978)
XLA Ops:
  6.5 0.0 copy-start
  6.5 0.0 reduce-scatter.2.cloned.1.call-start
  6.5 57.6 %fusion = f32[4096,512]{1,0:T(8,128)} fusion(f32[1024,4096]{1,0:T(8,128)} %param.5, f32[512,1024]{1,0:T(8,128)} %param.3), kind=kOutput, calls=%fused_computation.9 | convolution fusion | flops 25769803776 | bytes 27262976 | tf_op jit(solution)/shard_map/dot_general | solution.py:37
  64.2 0.0 reduce-scatter.2.cloned.1.call-update
  64.2 0.0 copy-done
  64.2 3.0 collective-permute-start
  67.2 48.7 %collective-permute-done = f32[512,1024]{1,0:T(8,128)S(1)} collective-permute-done((f32[512,1024]{1,0:T(8,128)S(1)}, f32[512,1024]{1,0:T(8,128)S(1)}, u32[]{:S(2)}, u32[]{:S(2)}) %collective-permute-start) | collective-permute-done | bytes 2097184 | tf_op jit(solution)/shard_map/ppermute | solution.py:22
  115.9 0.0 copy-start.1
  115.9 1.3 copy-done.1
  117.2 0.0 collective-permute-start.1
  117.2 49.5 %collective-permute-done.1 = f32[512,1024]{1,0:T(8,128)S(1)} collective-permute-done((f32[512,1024]{1,0:T(8,128)S(1)}, f32[512,1024]{1,0:T(8,128)S(1)}, u32[]{:S(2)}, u32[]{:S(2)}) %collective-permute-start.1) | collective-permute-done | bytes 2097184 | tf_op jit(solution)/shard_map/ppermute | solution.py:22
  166.7 0.0 copy-start.3
  166.7 1.3 copy-done.3
  168.0 0.0 collective-permute-start.2
  168.0 48.6 %collective-permute-done.2 = f32[512,1024]{1,0:T(8,128)S(1)} collective-permute-done((f32[512,1024]{1,0:T(8,128)S(1)}, f32[512,1024]{1,0:T(8,128)S(1)}, u32[]{:S(2)}, u32[]{:S(2)}) %collective-permute-start.2) | collective-permute-done | bytes 2097184 | tf_op jit(solution)/shard_map/ppermute | solution.py:22
  216.6 0.0 copy-start.5
  216.6 1.4 copy-done.5
  218.0 0.0 collective-permute-start.3
  218.1 47.8 %collective-permute-done.3 = f32[512,1024]{1,0:T(8,128)S(1)} collective-permute-done((f32[512,1024]{1,0:T(8,128)S(1)}, f32[512,1024]{1,0:T(8,128)S(1)}, u32[]{:S(2)}, u32[]{:S(2)}) %collective-permute-start.3) | collective-permute-done | bytes 2097184 | tf_op jit(solution)/shard_map/ppermute | solution.py:22
  265.8 0.0 copy-start.7
  265.8 1.3 copy-done.7
  267.1 0.0 collective-permute-start.4
  267.1 46.9 %collective-permute-done.4 = f32[512,1024]{1,0:T(8,128)S(1)} collective-permute-done((f32[512,1024]{1,0:T(8,128)S(1)}, f32[512,1024]{1,0:T(8,128)S(1)}, u32[]{:S(2)}, u32[]{:S(2)}) %collective-permute-start.4) | collective-permute-done | bytes 2097184 | tf_op jit(solution)/shard_map/ppermute | solution.py:22
  314.1 0.0 copy-start.9
  314.1 1.3 copy-done.9
  315.4 0.0 collective-permute-start.5
  315.4 46.2 %collective-permute-done.5 = f32[512,1024]{1,0:T(8,128)} collective-permute-done((f32[512,1024]{1,0:T(8,128)S(1)}, f32[512,1024]{1,0:T(8,128)}, u32[]{:S(2)}, u32[]{:S(2)}) %collective-permute-start.5) | collective-permute-done | bytes 2097184 | tf_op jit(solution)/shard_map/ppermute | solution.py:22
  361.5 0.0 collective-permute-start.6
  361.5 0.0 copy-start.2
  361.6 0.0 copy-start.4
  361.6 0.0 copy-start.6
  361.6 0.0 copy-start.8
  361.6 0.0 copy-start.10
  361.6 8.7 %broadcast_in_dim.3 = f32[4096,1024]{1,0:T(8,128)} broadcast(f32[]{:T(128)} %constant.56.clone.1), dimensions={} | broadcast | bytes 16777220 | tf_op jit(solution)/shard_map/broadcast_in_dim | solution.py:15
  370.3 1.6 constant_dynamic-update-slice_fusion.7
  371.9 0.0 copy-done.2
  371.9 1.4 constant_dynamic-update-slice_fusion.6
  373.3 0.0 copy-done.4
  373.4 1.5 constant_dynamic-update-slice_fusion.5
  374.8 0.0 copy-done.6
  374.8 1.5 constant_dynamic-update-slice_fusion.4
  376.3 0.0 copy-done.8
  376.3 1.5 constant_dynamic-update-slice_fusion.3
  377.8 0.0 copy-done.10
  377.8 1.5 constant_dynamic-update-slice_fusion.2
  379.3 3.2 constant_dynamic-update-slice_fusion.1
  382.5 24.6 %collective-permute-done.6 = f32[512,1024]{1,0:T(8,128)} collective-permute-done((f32[512,1024]{1,0:T(8,128)}, f32[512,1024]{1,0:T(8,128)}, u32[]{:S(2)}, u32[]{:S(2)}) %collective-permute-start.6) | collective-permute-done | bytes 2097184 | tf_op jit(solution)/shard_map/ppermute | solution.py:22
  407.1 3.2 constant_dynamic-update-slice_fusion
  410.2 0.0 reduce-scatter.2.cloned.1.call-done
  410.2 56.3 %add_bitcast_fusion = f32[512,1024]{0,1:T(8,128)S(1)} fusion(f32[1024,512]{1,0:T(8,128)} %reduce-scatter.2.cloned.1.call-done, f32[4096,1024]{1,0:T(8,128)} %constant_dynamic-update-slice_fusion, f32[512,4096]{1,0:T(8,128)} %param.4), kind=kOutput, calls=%fused_computation | convolution fusion | flops 25770328064 | bytes 29360128 | tf_op jit(solution)/shard_map/dot_general | solution.py:32
  466.6 1.8 copy.4
Async XLA Ops:
  6.5 57.7 %copy-start = (f32[512,1024]{1,0:T(8,128)S(1)}, f32[512,1024]{1,0:T(8,128)}, u32[]{:S(2)}) copy-start(f32[512,1024]{1,0:T(8,128)} %param.3) | copy-start | bytes 6291460
  6.5 403.7 %reduce-scatter.2.cloned.1.call-start = ((), (), s32[]{:S(2)}) async-start(), calls=%async_computation.1 | async-start | bytes 10485760 | tf_op jit(solution)/shard_map/reduce_scatter | solution.py:36
  64.2 51.7 %collective-permute-start = (f32[512,1024]{1,0:T(8,128)S(1)}, f32[512,1024]{1,0:T(8,128)S(1)}, u32[]{:S(2)}, u32[]{:S(2)}) collective-permute-start(f32[512,1024]{1,0:T(8,128)S(1)} %copy-done), channel_id=1, source_target_pairs={{0,4},{4,8},{8,12},{12,16},{16,20},{20,24},{24,28},{28,0},{1,5},{5... | collective-permute-start | bytes 6291464 | tf_op jit(solution)/shard_map/ppermute | solution.py:22
  115.9 1.3 copy-start.1
  117.2 49.5 %collective-permute-start.1 = (f32[512,1024]{1,0:T(8,128)S(1)}, f32[512,1024]{1,0:T(8,128)S(1)}, u32[]{:S(2)}, u32[]{:S(2)}) collective-permute-start(f32[512,1024]{1,0:T(8,128)S(1)} %collective-permute-done), channel_id=1, source_target_pairs={{0,4},{4,8},{8,12},{12,16},{16,20},{20,24},{24,28},{28,0},{1,5},{5... | collective-permute-start | bytes 6291464 | tf_op jit(solution)/shard_map/ppermute | solution.py:22
  166.7 1.3 copy-start.3
  168.0 48.6 %collective-permute-start.2 = (f32[512,1024]{1,0:T(8,128)S(1)}, f32[512,1024]{1,0:T(8,128)S(1)}, u32[]{:S(2)}, u32[]{:S(2)}) collective-permute-start(f32[512,1024]{1,0:T(8,128)S(1)} %collective-permute-done.1), channel_id=1, source_target_pairs={{0,4},{4,8},{8,12},{12,16},{16,20},{20,24},{24,28},{28,0},{1,5},{5... | collective-permute-start | bytes 6291464 | tf_op jit(solution)/shard_map/ppermute | solution.py:22
  216.6 1.4 copy-start.5
  218.0 47.8 %collective-permute-start.3 = (f32[512,1024]{1,0:T(8,128)S(1)}, f32[512,1024]{1,0:T(8,128)S(1)}, u32[]{:S(2)}, u32[]{:S(2)}) collective-permute-start(f32[512,1024]{1,0:T(8,128)S(1)} %collective-permute-done.2), channel_id=1, source_target_pairs={{0,4},{4,8},{8,12},{12,16},{16,20},{20,24},{24,28},{28,0},{1,5},{5... | collective-permute-start | bytes 6291464 | tf_op jit(solution)/shard_map/ppermute | solution.py:22
  265.8 1.3 copy-start.7
  267.1 46.9 %collective-permute-start.4 = (f32[512,1024]{1,0:T(8,128)S(1)}, f32[512,1024]{1,0:T(8,128)S(1)}, u32[]{:S(2)}, u32[]{:S(2)}) collective-permute-start(f32[512,1024]{1,0:T(8,128)S(1)} %collective-permute-done.3), channel_id=1, source_target_pairs={{0,4},{4,8},{8,12},{12,16},{16,20},{20,24},{24,28},{28,0},{1,5},{5... | collective-permute-start | bytes 6291464 | tf_op jit(solution)/shard_map/ppermute | solution.py:22
  314.1 1.3 copy-start.9
  315.4 46.2 %collective-permute-start.5 = (f32[512,1024]{1,0:T(8,128)S(1)}, f32[512,1024]{1,0:T(8,128)}, u32[]{:S(2)}, u32[]{:S(2)}) collective-permute-start(f32[512,1024]{1,0:T(8,128)S(1)} %collective-permute-done.4), channel_id=1, source_target_pairs={{0,4},{4,8},{8,12},{12,16},{16,20},{20,24},{24,28},{28,0},{1,5},{5... | collective-permute-start | bytes 6291464 | tf_op jit(solution)/shard_map/ppermute | solution.py:22
  361.5 45.5 %collective-permute-start.6 = (f32[512,1024]{1,0:T(8,128)}, f32[512,1024]{1,0:T(8,128)}, u32[]{:S(2)}, u32[]{:S(2)}) collective-permute-start(f32[512,1024]{1,0:T(8,128)} %collective-permute-done.5), channel_id=1, source_target_pairs={{0,4},{4,8},{8,12},{12,16},{16,20},{20,24},{24,28},{28,0},{1,5},{5... | collective-permute-start | bytes 6291464 | tf_op jit(solution)/shard_map/ppermute | solution.py:22
  361.5 10.4 %copy-start.2 = (f32[512,1024]{1,0:T(8,128)S(1)}, f32[512,1024]{1,0:T(8,128)}, u32[]{:S(2)}) copy-start(f32[512,1024]{1,0:T(8,128)} %copy-done.1) | copy-start | bytes 6291460
  361.6 11.8 %copy-start.4 = (f32[512,1024]{1,0:T(8,128)S(1)}, f32[512,1024]{1,0:T(8,128)}, u32[]{:S(2)}) copy-start(f32[512,1024]{1,0:T(8,128)} %copy-done.3) | copy-start | bytes 6291460
  361.6 13.3 %copy-start.6 = (f32[512,1024]{1,0:T(8,128)S(1)}, f32[512,1024]{1,0:T(8,128)}, u32[]{:S(2)}) copy-start(f32[512,1024]{1,0:T(8,128)} %copy-done.5) | copy-start | bytes 6291460
  361.6 14.7 %copy-start.8 = (f32[512,1024]{1,0:T(8,128)S(1)}, f32[512,1024]{1,0:T(8,128)}, u32[]{:S(2)}) copy-start(f32[512,1024]{1,0:T(8,128)} %copy-done.7) | copy-start | bytes 6291460
  361.6 16.3 %copy-start.10 = (f32[512,1024]{1,0:T(8,128)S(1)}, f32[512,1024]{1,0:T(8,128)}, u32[]{:S(2)}) copy-start(f32[512,1024]{1,0:T(8,128)} %copy-done.9) | copy-start | bytes 6291460
Sparse Core Ops, SparseCore 0:
  64.3 74.1 reduce-scatter.1
